TPU v7x, 512 devices: a whole 4x8x8 slice. The times are simulated.
512 devices in a mesh: seq: 64 (over x, y, core), head: 8 (over z).
Axes of the slice: x: 4, y: 8, z: 8, core: 2. Of those that a mesh axis runs over, the one named last changes fastest.
Arguments:
- query_feat: bfloat16 [32768, 512], P('seq', 'head'), may hold values from -6 to 6
- key_feat: bfloat16 [32768, 512], P('seq', 'head'), may hold values from -6 to 6
- values: bfloat16 [32768, 4096], P('seq', 'head'), may hold values from -6 to 6
- conv_query: float32 [3, 512], P(None, 'head'), may hold values from -3 to 3
- conv_key: float32 [3, 512], P(None, 'head'), may hold values from -3 to 3
- conv_value: float32 [3, 4096], P(None, 'head'), may hold values from -3 to 3
- norm_gain: float32 [4096], P('head'), may hold values from 0.1 to 1.9
- out_weight: bfloat16 [4096, 4096], P('head', 'seq'), may hold values from -0.09375 to 0.09375
- stream_ids: int32 [64], replicated, may hold values from 0 to 7, never falling along the last dimension, each value on 1 to 32 neighbouring positions
Outputs:
- mixed: bfloat16 [32768, 4096], P('seq', 'head')
Inputs may be any that keep to these rules, and one draw needn't show every extreme that they name: `stream_ids`: stream ids never fall along the shards; each stream holds 1 to 32 consecutive shards, and one stream holds exactly 32.
All inputs are finite; a program needn't handle non-finite values.
Results may differ from a plain program's by a relative error of at most 0.018.
Values may be sent and summed in bfloat16 or wider, within the bound.
A program may use at most 128 MiB of HBM per device.

v0:
```python
import numpy as np
import jax
import jax.numpy as jnp
from jax import lax
from jax.sharding import PartitionSpec as P

HD = 128
FEAT = 16
PAD = 160


def tables(heads):
    left = np.zeros((heads * FEAT, heads * PAD), np.float32)
    right = np.zeros((heads * FEAT, heads * PAD), np.float32)
    add_left = np.zeros((1, heads * PAD), np.float32)
    add_right = np.zeros((1, heads * PAD), np.float32)
    scale = np.zeros((1, heads * PAD), np.float32)
    twice = np.zeros((1, heads * PAD), np.float32)
    for h in range(heads):
        at = h * PAD
        add_left[0, at] = add_right[0, at] = scale[0, at] = twice[0, at] = 1.0
        for i in range(FEAT):
            at = h * PAD + 1 + i
            left[h * FEAT + i, at] = 1.0
            add_right[0, at] = scale[0, at] = twice[0, at] = 1.0
        at = h * PAD + 1 + FEAT
        for i in range(FEAT):
            for j in range(i, FEAT):
                left[h * FEAT + i, at] = 1.0
                right[h * FEAT + j, at] = 1.0
                scale[0, at] = np.float32(0.5**0.5)
                twice[0, at] = 1.0 if i == j else 2.0
                at += 1
    return (left, right, add_left, add_right, scale, twice)


def taylor(conv, heads):
    left, right, add_left, add_right, scale, twice = tables(heads)
    a = (conv.astype(jnp.float32) * FEAT ** (-0.25)).astype(jnp.bfloat16)
    one = jnp.dot(a, jnp.asarray(left, jnp.bfloat16), preferred_element_type=jnp.float32) + add_left
    two = (
        jnp.dot(a, jnp.asarray(right, jnp.bfloat16), preferred_element_type=jnp.float32) + add_right
    )
    return ((one * two * scale).astype(jnp.bfloat16), jnp.asarray(twice, jnp.bfloat16))


def convolve(inputs, rim_rows, kernel, keep):
    padded = jnp.concatenate(
        [rim_rows.astype(jnp.float32) * keep, inputs.astype(jnp.float32)], axis=0
    )
    return (kernel[0] * padded[:-2] + kernel[1] * padded[1:-1] + kernel[2] * padded[2:]).astype(
        jnp.bfloat16
    )


def on_device(
    query_feat,
    key_feat,
    values,
    conv_query,
    conv_key,
    conv_value,
    norm_gain,
    out_weight,
    stream_ids,
):
    rows, qw = query_feat.shape
    heads = values.shape[1] // HD
    shards = lax.axis_size("seq")
    weight = lax.all_gather(out_weight.T, "seq", axis=0, tiled=True)
    position = lax.axis_index("seq")
    own_stream = stream_ids[position]
    prior_stream = stream_ids[jnp.maximum(position - 1, 0)]
    keep = 1.0 - jnp.logical_or(position == 0, own_stream != prior_stream).astype(jnp.float32)
    rim = jnp.concatenate([query_feat[-2:], key_feat[-2:], values[-2:]], axis=1)
    rim = lax.ppermute(rim, "seq", [(i, i + 1) for i in range(shards - 1)])
    qconv = convolve(query_feat, rim[:, :qw], conv_query, keep)
    kconv = convolve(key_feat, rim[:, qw : 2 * qw], conv_key, keep)
    vconv = convolve(values, rim[:, 2 * qw :], conv_value, keep)
    phk, twice = taylor(kconv, heads)
    kv = [
        lax.dot_general(
            phk[:, h * PAD : (h + 1) * PAD],
            vconv[:, h * HD : (h + 1) * HD],
            (((0,), (0,)), ((), ())),
            preferred_element_type=jnp.float32,
        )
        for h in range(heads)
    ]
    pieces = jnp.concatenate(kv, axis=0).astype(jnp.bfloat16).reshape(shards, -1, HD)
    pieces = lax.all_to_all(pieces, "seq", 0, 0, tiled=True)
    order = jnp.arange(shards)
    earlier = (stream_ids[:, None] == stream_ids[None, :]) & (order[None, :] < order[:, None])
    sums = jnp.einsum(
        "ds,skl->dkl", earlier.astype(jnp.bfloat16), pieces, preferred_element_type=jnp.float32
    ).astype(jnp.bfloat16)
    state = lax.all_to_all(sums, "seq", 0, 0, tiled=True).reshape(heads, PAD, HD)
    phq, _ = taylor(qconv, heads)
    phq = phq * twice
    causal = jnp.tril(jnp.ones((rows, rows), jnp.bool_))
    hidden = []
    for h in range(heads):
        q = phq[:, h * PAD : (h + 1) * PAD]
        k = phk[:, h * PAD : (h + 1) * PAD]
        v = vconv[:, h * HD : (h + 1) * HD]
        scores = lax.dot_general(q, k, (((1,), (1,)), ((), ())), preferred_element_type=jnp.float32)
        scores = jnp.where(causal, scores, 0.0).astype(jnp.bfloat16)
        y = jnp.dot(scores, v, preferred_element_type=jnp.float32) + jnp.dot(
            q, state[h], preferred_element_type=jnp.float32
        )
        gain = norm_gain[h * HD : (h + 1) * HD]
        y = y * lax.rsqrt(jnp.mean(y * y, axis=-1, keepdims=True) + 1e-05) * gain
        hidden.append(y.astype(jnp.bfloat16))
    hidden = jnp.concatenate(hidden, axis=1)
    terms = lax.dot_general(
        hidden, weight, (((1,), (1,)), ((), ())), preferred_element_type=jnp.float32
    )
    return lax.psum_scatter(terms.astype(jnp.bfloat16), "head", scatter_dimension=1, tiled=True)


def solution(mesh):
    placed = (
        P("seq", "head"),
        P("seq", "head"),
        P("seq", "head"),
        P(None, "head"),
        P(None, "head"),
        P(None, "head"),
        P("head"),
        P("head", "seq"),
        P(),
    )
    return jax.shard_map(
        on_device, mesh=mesh, in_specs=placed, out_specs=P("seq", "head"), check_vma=False
    )
```

profile of v0, /device:TPU:1, one launch (start us, length us, event | category | flops | bytes accessed | tf_op | source)
XLA Modules:
  0.0 170.8 jit_solution(12257114810949976883)
XLA Ops:
  6.5 0.7 all-gather.2.cloned.1.call-update
  7.3 0.7 slice.138
  8.0 0.8 slice.136
  8.8 0.8 slice.137
  9.8 4.6 %collective-permute-start = (bf16[2,640]{1,0:T(2,128)(2,1)S(1)}, bf16[2,640]{1,0:T(2,128)(2,1)S(1)}, u32[]{:S(2)}, u32[]{:S(2)}) collective-permute-start(bf16[2,640]{1,0:T(2,128)(2,1)S(1)} %pad_maximum_fusion.4), channel_id=1, source_target_pairs={{0,8},{8,16},{16,24},{24,32},{32,40},{40,48},{48,56},{56,64},{64,7... | collective-permute-start | bytes 7688 | tf_op jit(solution)/shard_map/ppermute | solution.py:76
  14.4 0.8 slice_bitcast_fusion.5
  15.2 0.8 fusion.90
  16.0 0.8 fusion.89
  16.9 0.8 slice_bitcast_fusion.2
  17.7 0.8 convert_element_type.86
  18.5 0.9 convert_element_type.92
  19.4 1.2 convert_element_type.99
  20.5 0.7 fusion.91
  25.6 0.8 convert_element_type.101
  26.4 9.3 %all-to-all-start = ((bf16[64,10,128]{2,1,0:T(8,128)(2,1)}), bf16[64,10,128]{2,1,0:T(8,128)(2,1)S(1)}, u32[]{:S(2)}, u32[]{:S(2)}) async-start(bf16[64,10,128]{2,1,0:T(8,128)(2,1)} %convert_element_type.101), calls=%async_computation | async-start | bytes 524288 | tf_op jit(solution)/shard_map/all_to_all | solution.py:91
  37.2 0.6 fusion.12
  37.9 10.6 %all-to-all-done = bf16[64,10,128]{2,1,0:T(8,128)(2,1)S(1)} async-done(((bf16[64,10,128]{2,1,0:T(8,128)(2,1)}), bf16[64,10,128]{2,1,0:T(8,128)(2,1)S(1)}, u32[]{:S(2)}, u32[]{:S(2)}) %all-to-all-start) | async-done | bytes 163872 | tf_op jit(solution)/shard_map/all_to_all | solution.py:91
  48.7 0.8 copy.40
  49.5 5.9 %all-to-all-start.1 = ((bf16[64,10,128]{2,1,0:T(8,128)(2,1)}), bf16[64,10,128]{2,1,0:T(8,128)(2,1)S(1)}, u32[]{:S(2)}, u32[]{:S(2)}) async-start(bf16[64,10,128]{2,1,0:T(8,128)(2,1)} %copy.40), calls=%async_computation.1 | async-start | bytes 524288 | tf_op jit(solution)/shard_map/all_to_all | solution.py:97
  55.5 0.6 fusion.13
  56.7 10.7 %all-to-all-done.1 = bf16[64,10,128]{2,1,0:T(8,128)(2,1)S(1)} async-done(((bf16[64,10,128]{2,1,0:T(8,128)(2,1)}), bf16[64,10,128]{2,1,0:T(8,128)(2,1)S(1)}, u32[]{:S(2)}, u32[]{:S(2)}) %all-to-all-start.1) | async-done | bytes 163872 | tf_op jit(solution)/shard_map/all_to_all | solution.py:97
  69.1 32.4 %all-gather.2.cloned.1.call-done = bf16[4096,512]{1,0:T(8,128)(2,1)} async-done(((bf16[64,512]{1,0:T(8,128)(2,1)}), bf16[4096,512]{1,0:T(8,128)(2,1)}) %all-gather.2.cloned.1.call-update) | async-done | bytes 4194320 | tf_op jit(solution)/shard_map/all_gather | solution.py:70
  101.5 6.6 %convolution_convert_fusion = bf16[512,4096]{1,0:T(8,128)(2,1)} fusion(bf16[4096,512]{1,0:T(8,128)(2,1)} %all-gather.2.cloned.1.call-done, bf16[512,128]{0,1:T(8,128)(2,1)S(1)} %get-tuple-element.34, bf16[512,128]{0,1:T(8,128)(2,1)S(1)} %get-tuple-element.35, bf16[512,128]{0,1:T(8,128)(2,1)S(1)} %get-tuple-element.36, bf16[512,128]{0,1:T(8,128)(2,1)S(1)} %get-tuple-element.37), kind=kOutput, calls=%fused_computation | convolution fusion | flops 2151677952 | bytes 8912896 | tf_op jit(solution)/shard_map/dot_general | solution.py:115
  108.1 55.9 %reduce-scatter.2.cloned.1.call-done = bf16[512,512]{1,0:T(8,128)(2,1)} async-done(((bf16[512,4096]{1,0:T(8,128)(2,1)}), bf16[512,512]{1,0:T(8,128)(2,1)}) %reduce-scatter.2.cloned.1.call-update) | async-done | bytes 524304 | tf_op jit(solution)/shard_map/reduce_scatter | solution.py:118
  (55 shorter events, 7.1 us)
Async XLA Ops:
  6.5 16.5 %copy-start.4 = (f32[640]{0:T(1024)S(1)}, f32[640]{0:T(1024)}, u32[]{:S(2)}) copy-start(f32[640]{0:T(1024)} %constant.49) | copy-start | bytes 7684
  6.5 16.5 %copy-start.1 = (bf16[64,640]{1,0:T(8,128)(2,1)S(1)}, bf16[64,640]{1,0:T(8,128)(2,1)}, u32[]{:S(2)}) copy-start(bf16[64,640]{1,0:T(8,128)(2,1)} %constant.43.clone) | copy-start | bytes 245764
  6.5 14.0 %copy-start.5 = (s32[64]{0:T(128)S(1)}, s32[64]{0:T(128)}, u32[]{:S(2)}) copy-start(s32[64]{0:T(128)} %param.28) | copy-start | bytes 772
  6.5 94.9 %all-gather.2.cloned.1.call-start = ((), (), s32[]{:S(2)}) async-start(), calls=%async_computation.3 | async-start | bytes 4259840 | tf_op jit(solution)/shard_map/all_gather | solution.py:70
  9.8 12.8 %collective-permute-start = (bf16[2,640]{1,0:T(2,128)(2,1)S(1)}, bf16[2,640]{1,0:T(2,128)(2,1)S(1)}, u32[]{:S(2)}, u32[]{:S(2)}) collective-permute-start(bf16[2,640]{1,0:T(2,128)(2,1)S(1)} %pad_maximum_fusion.4), channel_id=1, source_target_pairs={{0,8},{8,16},{16,24},{24,32},{32,40},{40,48},{48,56},{56,64},{64,7... | collective-permute-start | bytes 7688 | tf_op jit(solution)/shard_map/ppermute | solution.py:76
  23.1 0.9 copy-start
  23.1 0.9 copy-start.2
  23.1 0.9 copy-start.3
  25.6 10.7 %copy-start.6 = (bf16[640]{0:T(1024)(128)(2,1)S(1)}, bf16[640]{0:T(1024)(128)(2,1)}, u32[]{:S(2)}) copy-start(bf16[640]{0:T(1024)(128)(2,1)} %constant.52) | copy-start | bytes 3844
  26.4 22.1 %all-to-all-start = ((bf16[64,10,128]{2,1,0:T(8,128)(2,1)}), bf16[64,10,128]{2,1,0:T(8,128)(2,1)S(1)}, u32[]{:S(2)}, u32[]{:S(2)}) async-start(bf16[64,10,128]{2,1,0:T(8,128)(2,1)} %convert_element_type.101), calls=%async_computation | async-start | bytes 524288 | tf_op jit(solution)/shard_map/all_to_all | solution.py:91
  49.5 17.9 %all-to-all-start.1 = ((bf16[64,10,128]{2,1,0:T(8,128)(2,1)}), bf16[64,10,128]{2,1,0:T(8,128)(2,1)S(1)}, u32[]{:S(2)}, u32[]{:S(2)}) async-start(bf16[64,10,128]{2,1,0:T(8,128)(2,1)} %copy.40), calls=%async_computation.1 | async-start | bytes 524288 | tf_op jit(solution)/shard_map/all_to_all | solution.py:97
  55.5 108.5 %reduce-scatter.2.cloned.1.call-start = ((), (), s32[]{:S(2)}) async-start(), calls=%async_computation.4 | async-start | bytes 4718592 | tf_op jit(solution)/shard_map/reduce_scatter | solution.py:118
Sparse Core Ops, SparseCore 0:
  10.7 90.7 all-gather.1
  108.2 55.7 reduce-scatter.1
where the time goes:
time: 172 us; the launch traced here: 171 us
  waiting for transfers between devices  110 us (64%)
  starting transfers between devices  19.9 us (12%)
  between operations  15 us (9%)
  matrix products  13.1 us (8%)
  local copies, waits for them, and re-layouts  8.47 us (5%)
  other arithmetic  3.95 us (2%)
    reduce_scatter x1, waiting for transfers between devices, on_device(): lax.psum_scatter(terms.astype(jnp.bfloat16), 'head', scatter_dimension=1,...  55.9 us
    all_gather x1, waiting for transfers between devices, on_device(): weight = lax.all_gather(out_weight.T, 'seq', axis=0, tiled=True)  32.4 us
    all_to_all x1, waiting for transfers between devices, on_device(): lax.all_to_all(sums, 'seq', 0, 0, tiled=True).reshape(heads, PAD, HD)  10.7 us
    all_to_all x1, waiting for transfers between devices, on_device(): pieces = lax.all_to_all(pieces, 'seq', 0, 0, tiled=True)  10.6 us
    all_to_all x1, starting transfers between devices, on_device(): pieces = lax.all_to_all(pieces, 'seq', 0, 0, tiled=True)  9.33 us
    dot_general x1, matrix products, on_device(): lax.dot_general(hidden, weight, (((1,), (1,)), ((), ())), preferred_eleme...  6.57 us
    all_to_all x1, starting transfers between devices, on_device(): lax.all_to_all(sums, 'seq', 0, 0, tiled=True).reshape(heads, PAD, HD)  5.94 us
    ppermute x1, starting transfers between devices, on_device(): rim = lax.ppermute(rim, 'seq', [(i, i + 1) for i in range(shards - 1)])  4.58 us
  transfers between devices with their start and end apart: 5, of which 4 were waited for; matrix products, arithmetic and copies ran while one was open for 11% of the time, Pallas kernels for 0%

commit v1 on v0

--- a/solution.py
+++ b/solution.py
@@ -67,7 +67,9 @@
     rows, qw = query_feat.shape
     heads = values.shape[1] // HD
     shards = lax.axis_size("seq")
-    weight = lax.all_gather(out_weight.T, "seq", axis=0, tiled=True)
+    weight = jnp.concatenate(
+        lax.all_to_all(jnp.stack([out_weight.T] * lax.axis_size("seq")), "seq", 0, 0), axis=0
+    )
     position = lax.axis_index("seq")
     own_stream = stream_ids[position]
     prior_stream = stream_ids[jnp.maximum(position - 1, 0)]

time: 172 us -> 239 us (1.39)
  waiting for transfers between devices: 110 us -> 149 us
  blocking collectives: 0 us -> 38.9 us
  starting transfers between devices: 19.9 us -> 11.2 us
    all_to_all x2 -> x1, waiting for transfers between devices: 21.3 us -> 90.4 us  [on_device(): lax.all_to_all(jnp.stack([out_weight.T] * lax.axis_size('seq')), 'seq', 0...]
    all_to_all x0 -> x2, blocking collectives: none -> 38.9 us  [the longest x1 21.1 us: on_device(): pieces = lax.all_to_all(pieces, 'seq', 0, 0, tiled=True)]
    all_gather x1 -> x0, waiting for transfers between devices: 32.4 us -> none  [on_device(): weight = lax.all_gather(out_weight.T, 'seq', axis=0, tiled=True)]
    all_to_all x2 -> x1, starting transfers between devices: 15.3 us -> 6.36 us  [on_device(): lax.all_to_all(jnp.stack([out_weight.T] * lax.axis_size('seq')), 'seq', 0...]
    reduce_scatter x1, waiting for transfers between devices: 55.9 us -> 58.5 us  [on_device(): lax.psum_scatter(terms.astype(jnp.bfloat16), 'head', scatter_dimension=1,...]
    another operation x0 -> x1, local copies, waits for them, and re-layouts: none -> 2.47 us  [on_device(): jnp.stack([out_weight.T] * lax.axis_size('seq'))]
  transfers between devices with their start and end apart: 5 -> 3, of which waited for: 4 -> 2; matrix products, arithmetic and copies ran while one was open for 11% -> 4% of each run, Pallas kernels for 0% -> 0%
where the time goes in v1:
time: 239 us; the launch traced here: 238 us
  waiting for transfers between devices  149 us (62%)
  blocking collectives  38.9 us (16%)
  between operations  15.1 us (6%)
  matrix products  13.1 us (5%)
  starting transfers between devices  11.2 us (5%)
  local copies, waits for them, and re-layouts  7.8 us (3%)
  other arithmetic  3.15 us (1%)
    all_to_all x1, waiting for transfers between devices, on_device(): lax.all_to_all(jnp.stack([out_weight.T] * lax.axis_size('seq')), 'seq', 0...  90.4 us
    reduce_scatter x1, waiting for transfers between devices, on_device(): lax.psum_scatter(terms.astype(jnp.bfloat16), 'head', scatter_dimension=1,...  58.5 us
    all_to_all x1, blocking collectives, on_device(): pieces = lax.all_to_all(pieces, 'seq', 0, 0, tiled=True)  21.1 us
    all_to_all x1, blocking collectives, on_device(): lax.all_to_all(sums, 'seq', 0, 0, tiled=True).reshape(heads, PAD, HD)  17.8 us
    dot_general x1, matrix products, on_device(): lax.dot_general(hidden, weight, (((1,), (1,)), ((), ())), preferred_eleme...  6.56 us
    all_to_all x1, starting transfers between devices, on_device(): lax.all_to_all(jnp.stack([out_weight.T] * lax.axis_size('seq')), 'seq', 0...  6.36 us
  transfers between devices with their start and end apart: 3, of which 2 were waited for; matrix products, arithmetic and copies ran while one was open for 4% of the time, Pallas kernels for 0%

profile of v1, /device:TPU:1, one launch (start us, length us, event | category | flops | bytes accessed | tf_op | source)
XLA Modules:
  0.0 238.1 jit_solution(10450783701088562006)
XLA Ops:
  6.5 0.7 slice.138
  7.3 0.8 slice.137
  8.2 0.8 slice.136
  9.1 4.6 %collective-permute-start = (bf16[2,640]{1,0:T(2,128)(2,1)S(1)}, bf16[2,640]{1,0:T(2,128)(2,1)S(1)}, u32[]{:S(2)}, u32[]{:S(2)}) collective-permute-start(bf16[2,640]{1,0:T(2,128)(2,1)S(1)} %pad_maximum_fusion.4), channel_id=1, source_target_pairs={{0,8},{8,16},{16,24},{24,32},{32,40},{40,48},{48,56},{56,64},{64,7... | collective-permute-start | bytes 7688 | tf_op jit(solution)/shard_map/ppermute | solution.py:78
  13.7 0.8 fusion.89
  14.6 0.8 slice_bitcast_fusion.2
  15.3 0.8 convert_element_type.92
  16.2 1.2 convert_element_type.99
  17.5 0.7 fusion.91
  19.8 0.3 convolution_add_fusion.1
  20.2 0.4 fusion.5
  22.2 21.1 %all_to_all.15 = bf16[64,10,128]{2,1,0:T(8,128)(2,1)S(1)} all-to-all(bf16[64,10,128]{2,1,0:T(8,128)(2,1)S(1)} %convert_element_type.101), channel_id=1, replica_groups=mesh['seq'=64,'head'=8] {'seq'}, dimensions={0} | all-to-all | bytes 327680 | tf_op jit(solution)/shard_map/all_to_all | solution.py:93
  43.7 17.8 %all_to_all.16 = bf16[64,10,128]{2,1,0:T(8,128)(2,1)S(1)} all-to-all(bf16[64,10,128]{2,1,0:T(8,128)(2,1)S(1)} %copy.40), channel_id=1, replica_groups=mesh['seq'=64,'head'=8] {'seq'}, dimensions={0} | all-to-all | bytes 327680 | tf_op jit(solution)/shard_map/all_to_all | solution.py:99
  61.5 2.5 %stack.2 = bf16[64,64,512]{2,1,0:T(8,128)(2,1)} broadcast(bf16[64,512]{1,0:T(8,128)(2,1)S(1)} %bitcast.34), dimensions={1,2} | broadcast | bytes 4259840 | tf_op jit(solution)/shard_map/stack | solution.py:71
  64.0 6.4 %all-to-all-start.2 = ((bf16[64,64,512]{2,1,0:T(8,128)(2,1)}), bf16[64,64,512]{2,1,0:T(8,128)(2,1)}, u32[]{:S(2)}, u32[]{:S(2)}) async-start(bf16[64,64,512]{2,1,0:T(8,128)(2,1)} %stack.2), calls=%async_computation.2 | async-start | bytes 8388608 | tf_op jit(solution)/shard_map/all_to_all | solution.py:71
  70.9 0.3 convolution_add_fusion.3
  71.3 0.4 fusion.10
  71.7 0.6 fusion.11
  72.3 0.6 fusion.12
  72.9 0.6 fusion.13
  73.5 0.6 fusion.14
  75.8 90.4 %all-to-all-done.2 = bf16[64,64,512]{2,1,0:T(8,128)(2,1)} async-done(((bf16[64,64,512]{2,1,0:T(8,128)(2,1)}), bf16[64,64,512]{2,1,0:T(8,128)(2,1)}, u32[]{:S(2)}, u32[]{:S(2)}) %all-to-all-start.2) | async-done | bytes 4194336 | tf_op jit(solution)/shard_map/all_to_all | solution.py:71
  166.2 6.6 %convolution_convert_fusion = bf16[512,4096]{1,0:T(8,128)(2,1)} fusion(bf16[4096,512]{1,0:T(8,128)(2,1)} %bitcast.12, bf16[512,128]{0,1:T(8,128)(2,1)S(1)} %get-tuple-element.34, bf16[512,128]{0,1:T(8,128)(2,1)S(1)} %get-tuple-element.35, bf16[512,128]{0,1:T(8,128)(2,1)S(1)} %get-tuple-element.36, bf16[512,128]{0,1:T(8,128)(2,1)S(1)} %get-tuple-element.37), kind=kOutput, calls=%fused_computation | convolution fusion | flops 2151677952 | bytes 8912896 | tf_op jit(solution)/shard_map/dot_general | solution.py:117
  172.8 58.5 %reduce-scatter.2.cloned.1.call-done = bf16[512,512]{1,0:T(8,128)(2,1)} async-done(((bf16[512,4096]{1,0:T(8,128)(2,1)}), bf16[512,512]{1,0:T(8,128)(2,1)}) %reduce-scatter.2.cloned.1.call-update) | async-done | bytes 524304 | tf_op jit(solution)/shard_map/reduce_scatter | solution.py:120
  (61 shorter events, 4.8 us)
Async XLA Ops:
  6.5 13.2 %copy-start.1 = (bf16[64,640]{1,0:T(8,128)(2,1)S(1)}, bf16[64,640]{1,0:T(8,128)(2,1)}, u32[]{:S(2)}) copy-start(bf16[64,640]{1,0:T(8,128)(2,1)} %constant.43.clone) | copy-start | bytes 245764
  6.5 13.2 %copy-start.6 = (f32[640]{0:T(1024)S(1)}, f32[640]{0:T(1024)}, u32[]{:S(2)}) copy-start(f32[640]{0:T(1024)} %constant.49) | copy-start | bytes 7684
  6.5 10.9 %copy-start.7 = (s32[64]{0:T(128)S(1)}, s32[64]{0:T(128)}, u32[]{:S(2)}) copy-start(s32[64]{0:T(128)} %param.28) | copy-start | bytes 772
  9.1 10.3 %collective-permute-start = (bf16[2,640]{1,0:T(2,128)(2,1)S(1)}, bf16[2,640]{1,0:T(2,128)(2,1)S(1)}, u32[]{:S(2)}, u32[]{:S(2)}) collective-permute-start(bf16[2,640]{1,0:T(2,128)(2,1)S(1)} %pad_maximum_fusion.4), channel_id=1, source_target_pairs={{0,8},{8,16},{16,24},{24,32},{32,40},{40,48},{48,56},{56,64},{64,7... | collective-permute-start | bytes 7688 | tf_op jit(solution)/shard_map/ppermute | solution.py:78
  16.2 3.9 %copy-start = (bf16[64,640]{1,0:T(8,128)(2,1)S(1)}, bf16[64,640]{1,0:T(8,128)(2,1)}, u32[]{:S(2)}) copy-start(bf16[64,640]{1,0:T(8,128)(2,1)} %constant.45.clone) | copy-start | bytes 245764
  16.2 3.9 %copy-start.4 = (f32[640]{0:T(1024)S(1)}, f32[640]{0:T(1024)}, u32[]{:S(2)}) copy-start(f32[640]{0:T(1024)} %constant.51) | copy-start | bytes 7684
  16.2 3.9 %copy-start.5 = (f32[640]{0:T(1024)S(1)}, f32[640]{0:T(1024)}, u32[]{:S(2)}) copy-start(f32[640]{0:T(1024)} %constant.50) | copy-start | bytes 7684
  22.1 39.4 %copy-start.3 = (bf16[512,64]{0,1:T(8,128)(2,1)S(1)}, bf16[512,64]{0,1:T(8,128)(2,1)}, u32[]{:S(2)}) copy-start(bf16[512,64]{0,1:T(8,128)(2,1)} %param.27) | copy-start | bytes 196612
  64.0 6.6 %copy-start.2 = (bf16[512,64]{0,1:T(8,128)(2,1)S(1)}, bf16[512,64]{0,1:T(8,128)(2,1)}, u32[]{:S(2)}) copy-start(bf16[512,64]{0,1:T(8,128)(2,1)} %param.20) | copy-start | bytes 196612
  64.0 6.6 %copy-start.10 = (f32[3,64]{1,0:T(4,128)S(1)}, f32[3,64]{1,0:T(4,128)}, u32[]{:S(2)}) copy-start(f32[3,64]{1,0:T(4,128)} %param.23) | copy-start | bytes 2308
  64.0 6.7 %copy-start.9 = (f32[512]{0:T(512)S(1)}, f32[512]{0:T(512)}, u32[]{:S(2)}) copy-start(f32[512]{0:T(512)} %param.26) | copy-start | bytes 6148
  64.0 102.2 %all-to-all-start.2 = ((bf16[64,64,512]{2,1,0:T(8,128)(2,1)}), bf16[64,64,512]{2,1,0:T(8,128)(2,1)}, u32[]{:S(2)}, u32[]{:S(2)}) async-start(bf16[64,64,512]{2,1,0:T(8,128)(2,1)} %stack.2), calls=%async_computation.2 | async-start | bytes 8388608 | tf_op jit(solution)/shard_map/all_to_all | solution.py:71
  70.3 0.9 copy-start.8
  70.4 160.9 %reduce-scatter.2.cloned.1.call-start = ((), (), s32[]{:S(2)}) async-start(), calls=%async_computation.4 | async-start | bytes 4718592 | tf_op jit(solution)/shard_map/reduce_scatter | solution.py:120
Sparse Core Ops, SparseCore 0:
  172.9 58.3 reduce-scatter.1
